TPU v7x, 512 devices: a whole 4x4x16 slice. The times are simulated.
512 devices in a mesh: req: 8 (over x, core), vocab: 64 (over y, z).
Axes of the slice: x: 4, y: 4, z: 16, core: 2. Of those that a mesh axis runs over, the one named last changes fastest.
Arguments:
- hidden: bfloat16 [8192, 2304], P(('req', 'vocab'))
- norm_gain: float32 [2304], replicated, may hold values from 0.5 to 1.5
- head_weight: bfloat16 [2304, 65536], P(None, 'vocab')
- targets: int32 [8192], P(('req', 'vocab')), may hold values from 0 to 65535
- counts: int32 [512], P(('req', 'vocab')), may hold values from 5 to 10, as said below
Outputs:
- logprob: float32 [8192], P(('req', 'vocab'))
- entropy: float32 [8192], P(('req', 'vocab'))
Inputs may be any that keep to these rules, and one draw needn't show every extreme that they name: The scored slots of a device are its first counts slots; some device holds exactly 10.
All inputs are finite; a program needn't handle non-finite values.
Results may differ from a plain program's by a relative error of at most 0.012.
The roundings to bfloat16 on the way count: a program that leaves them out, or rounds other values in their place, can miss the bound.
Values may be sent and summed in bfloat16 or wider, within the bound.
A program may use at most 64 MiB of HBM per device.

v0:
```python
import jax
import jax.numpy as jnp
from jax import lax
from jax.sharding import PartitionSpec as P

logit_scale = 256.0 / 2304.0


def on_device(hidden, norm_gain, head_weight, targets, counts):
    slots = hidden.shape[0]
    vocab_dev = head_weight.shape[1]
    values = hidden.astype(jnp.float32)
    square_mean = jnp.mean(values * values, axis=1, keepdims=True)
    normed = (values * lax.rsqrt(square_mean + 1e-05) * norm_gain[None, :]).astype(jnp.bfloat16)
    gathered = lax.all_gather(normed, "vocab", axis=0, tiled=True)
    wanted = lax.all_gather(targets, "vocab", axis=0, tiled=True)
    position = lax.axis_index("vocab")
    start = position * vocab_dev
    logits = jnp.dot(gathered, head_weight, preferred_element_type=jnp.float32) * logit_scale
    local_peak = jnp.max(logits, axis=1)
    weights = jnp.exp(logits - local_peak[:, None])
    local_total = jnp.sum(weights, axis=1)
    local_moment = jnp.sum(weights * logits, axis=1)
    columns = lax.broadcasted_iota(jnp.int32, logits.shape, 1)
    hits = columns == (wanted - start)[:, None]
    local_chosen = jnp.sum(jnp.where(hits, logits, jnp.float32(0.0)), axis=1)
    own_start = position * slots
    peak = lax.pmax(local_peak, "vocab")
    factor = jnp.exp(local_peak - peak)
    total, moment, chosen = lax.psum(
        (local_total * factor, local_moment * factor, local_chosen), "vocab"
    )
    peak = lax.dynamic_slice_in_dim(peak, own_start, slots, 0)
    total = lax.dynamic_slice_in_dim(total, own_start, slots, 0)
    moment = lax.dynamic_slice_in_dim(moment, own_start, slots, 0)
    chosen = lax.dynamic_slice_in_dim(chosen, own_start, slots, 0)
    log_total = jnp.log(total)
    row_logprob = chosen - peak - log_total
    row_entropy = peak + log_total - moment / total
    scored = jnp.arange(slots, dtype=jnp.int32) < counts[0]
    logprob = jnp.where(scored, row_logprob, jnp.float32(0.0))
    entropy = jnp.where(scored, row_entropy, jnp.float32(0.0))
    return (logprob, entropy)


def solution(mesh):
    in_specs = (
        P(("req", "vocab"), None),
        P(),
        P(None, "vocab"),
        P(("req", "vocab")),
        P(("req", "vocab")),
    )
    out_specs = (P(("req", "vocab")), P(("req", "vocab")))
    return jax.shard_map(
        on_device, mesh=mesh, in_specs=in_specs, out_specs=out_specs, check_vma=False
    )
```

profile of v0, /device:TPU:6, one launch (start us, length us, event | category | flops | bytes accessed | tf_op | source)
XLA Modules:
  0.0 597.7 jit_solution(12411785864831970918)
XLA Ops:
  7.2 0.0 all-gather.2.cloned.1.call-start
  7.2 1.0 fusion.1
  8.2 1.6 fusion.3
  9.8 0.0 all-gather.2.cloned.1.call-update
  10.5 1.3 dynamic-slice
  12.5 0.9 dynamic-update-slice
  13.3 34.4 %all-reduce = s32[1024]{0:T(1024)S(1)} all-reduce(s32[1024]{0:T(1024)S(1)} %dynamic-update-slice), channel_id=1, replica_groups=mesh['req'=8,'vocab'=64] {'vocab'}, use_global_device_ids=true, to_apply=%add | all-reduce | flops 1024 | bytes 8192
  47.7 115.1 %all-gather.2.cloned.1.call-done = bf16[1024,2304]{1,0:T(8,128)(2,1)} async-done(((bf16[16,2304]{1,0:T(8,128)(2,1)}), bf16[1024,2304]{1,0:T(8,128)(2,1)}) %all-gather.2.cloned.1.call-update) | async-done | bytes 4718608 | tf_op jit(solution)/shard_map/all_gather | solution.py:15
  162.8 9.8 %multiply_reduce_fusion.1 = (f32[1024]{0:T(1024)S(1)}, f32[1024,1024]{0,1:T(8,128)}) fusion(bf16[1024,2304]{1,0:T(8,128)(2,1)} %all-gather.2.cloned.1.call-done, bf16[2304,1024]{1,0:T(8,128)(2,1)} %param.7), kind=kOutput, calls=%fused_computation.5 | convolution fusion | flops 4833934336 | bytes 13635584 | tf_op jit(solution)/shard_map/dot_general | solution.py:19
  172.5 140.0 %pmax.7 = f32[1024]{0:T(1024)S(1)} all-reduce(f32[1024]{0:T(1024)S(1)} %get-tuple-element.12), channel_id=1, replica_groups=mesh['req'=8,'vocab'=64] {'vocab'}, use_global_device_ids=true, to_apply=%region_4.5 | all-reduce | flops 1024 | bytes 8192 | tf_op jit(solution)/shard_map/pmax | solution.py:28
  312.5 3.7 multiply_reduce_fusion
  316.3 274.0 %all-reduce.1 = (f32[1024]{0:T(1024)S(1)}, f32[1024]{0:T(1024)S(1)}, f32[1024]{0:T(1024)S(1)}) all-reduce(f32[1024]{0:T(1024)S(1)} %get-tuple-element.4, f32[1024]{0:T(1024)S(1)} %get-tuple-element.11, f32[1024]{0:T(1024)S(1)} %get-tuple-element.10), channel_id=1, replica_groups=mesh['req'=8,'vocab'=64] {'vocab'}, use_global_device_ids=true, to_apply=%region_2.0 | all-reduce | flops 3072 | bytes 24576 | tf_op jit(solution)/shard_map/psum | solution.py:30
  590.2 0.6 compare_select_fusion
  (4 shorter events, 0.0 us)
Async XLA Ops:
  7.2 155.6 %all-gather.2.cloned.1.call-start = ((), (), s32[]{:S(2)}) async-start(), calls=%async_computation | async-start | bytes 4792320 | tf_op jit(solution)/shard_map/all_gather | solution.py:15
Sparse Core Ops, SparseCore 0:
  10.9 151.8 all-gather.1
where the time goes:
time: 598 us
  blocking collectives  448 us (75%)
  waiting for transfers between devices  115 us (19%)
  between operations  15.4 us (3%)
  matrix products  9.76 us (2%)
  other arithmetic  6.94 us (1%)
    psum x1, blocking collectives, on_device(): lax.psum((local_total * factor, local_moment * factor, local_chosen), 'vo...  274 us
    pmax x1, blocking collectives, on_device(): peak = lax.pmax(local_peak, 'vocab')  140 us
    all_gather x1, waiting for transfers between devices, on_device(): gathered = lax.all_gather(normed, 'vocab', axis=0, tiled=True)  115 us
    unnamed x1, blocking collectives  34.4 us
  transfers between devices with their start and end apart: 1, of which 1 were waited for; matrix products, arithmetic and copies ran while one was open for 0% of the time, Pallas kernels for 0%

commit v1 on v0

v1 whole, which is shorter than its diff:
```python
import jax
import jax.numpy as jnp
from jax import lax
from jax.experimental import pallas as pl
from jax.experimental.pallas import tpu as pltpu
from jax.sharding import PartitionSpec as P

logit_scale = 256.0 / 2304.0
NY, NZ = 4, 16
CAP = 10
MAIN = 8
REST = CAP - MAIN
SPLIT = 1920
EXTRA = 128


def kernel(
    hidden_hbm, gain_hbm, weight_hbm, targets_ref, counts_ref,
    logprob_ref, entropy_ref,
    hid, gain, weight, za, yb, rl, rest32, block, logits, turn, stat_out, stat_in, sum_out, sum_in,
    local_sem, za_s, za_r, zb_s, zb_r, zr_s, zr_r, ya_s, ya_r, yh_s, yh_r,
    b0_s, b0_r, r0_s, r0_r, st_s, st_r, s2_s, s2_r,
):
    depth = hid.shape[1]
    half = (SPLIT // 256 + 1) // 1 * 128 if (SPLIT // 128) % 2 else SPLIT // 2
    vocab_dev = weight.shape[1]
    me = lax.axis_index("vocab")
    my_y, my_z = me // NZ, lax.rem(me, NZ)

    def at(y, z):
        return {"vocab": lax.rem(y + NY, NY) * NZ + lax.rem(z + NZ, NZ)}

    near = [at(my_y, my_z + 1), at(my_y, my_z - 1), at(my_y + 1, my_z), at(my_y - 1, my_z), at(my_y + 2, my_z)]
    barrier = pltpu.get_barrier_semaphore()
    for device in near:
        pl.semaphore_signal(barrier, inc=1, device_id=device, device_id_type=pl.DeviceIdType.MESH)
    fetch_hidden = pltpu.make_async_copy(hidden_hbm, hid, local_sem.at[0])
    fetch_gain = pltpu.make_async_copy(gain_hbm, gain, local_sem.at[1])
    fetch_weight = pltpu.make_async_copy(weight_hbm, weight, local_sem.at[2])
    fetch_hidden.start()
    fetch_gain.start()
    fetch_weight.start()

    def remote(src, dst, send, recv, device):
        return pltpu.make_async_remote_copy(
            src_ref=src, dst_ref=dst, send_sem=send, recv_sem=recv,
            device_id=device, device_id_type=pl.DeviceIdType.MESH,
        )

    def plane(way, hop):
        return hop if way == 0 else lax.rem(NZ - hop, NZ)

    def z_main(way, hop):
        src, dst = plane(way, hop - 1), plane(way, hop)
        return remote(za.at[src, 0], za.at[dst, 0], za_s.at[way, hop], za_r.at[way, hop], near[way])

    def z_main_half(way):
        last = NZ // 2
        cols = pl.ds(0, half) if way == 0 else pl.ds(half, SPLIT - half)
        src = plane(way, last - 1)
        return remote(
            za.at[src, 0, :, cols], za.at[last, 0, :, cols], za_s.at[way, last], za_r.at[way, last], near[way]
        )

    def z_side(way, hop):
        src, dst = plane(way, hop - 1), plane(way, hop)
        return [
            remote(rl.at[src], rl.at[dst], zr_s.at[way, hop], zr_r.at[way, hop], near[way]),
            remote(yb.at[src], yb.at[dst], zb_s.at[way, hop], zb_r.at[way, hop], near[way]),
        ]

    def z_side_half(way):
        last = NZ // 2
        src = plane(way, last - 1)
        part = pl.ds(0, NY // 2) if way == 0 else pl.ds(NY // 2, NY // 2)
        return [
            remote(rl.at[src, part], rl.at[last, part], zr_s.at[way, last], zr_r.at[way, last], near[way]),
            remote(yb.at[src, part], yb.at[last, part], zb_s.at[way, last], zb_r.at[way, last], near[way]),
        ]

    def y_main(p, way):
        slot = 1 if way == 0 else NY - 1
        return remote(za.at[p, 0], za.at[p, slot], ya_s.at[p, way], ya_r.at[p, way], near[2 + way])

    def y_half(p, way):
        slot = 1 if way == 0 else NY - 1
        cols = pl.ds(0, half) if way == 0 else pl.ds(half, SPLIT - half)
        return remote(
            za.at[p, slot, :, cols], za.at[p, 2, :, cols], yh_s.at[p, way], yh_r.at[p, way], near[2 + way]
        )

    y_near = {1: near[2], 2: near[4], 3: near[3]}

    def y_side(j):
        return [
            remote(rl.at[0, 0], rl.at[0, j], r0_s.at[j], r0_r.at[j], y_near[j]),
            remote(yb.at[0, 0], yb.at[0, j], b0_s.at[j], b0_r.at[j], y_near[j]),
        ]

    def stat_copy(p):
        device = at(my_y, my_z - p)
        return remote(stat_out.at[p], stat_in.at[p], st_s.at[p], st_r.at[p], device)

    def sum_copy(j):
        return remote(sum_out, sum_in.at[j], s2_s.at[j], s2_r.at[j], {1: near[3], 2: near[4], 3: near[2]}[j])

    def start(copies):
        for copy in copies:
            copy.start()

    def arrive(copies):
        for copy in copies:
            copy.wait_recv()

    fetch_hidden.wait()
    fetch_gain.wait()
    values = hid[...].astype(jnp.float32)
    square_mean = jnp.mean(values * values, axis=1, keepdims=True)
    normed = values * lax.rsqrt(square_mean + 1e-05) * gain[...]
    rows = normed.astype(jnp.bfloat16)
    za[0, 0] = rows[0:MAIN, 0:SPLIT]
    yb[0, 0] = rows[0:MAIN, SPLIT:depth]
    rl[0, 0, :, 0:depth] = normed[MAIN:CAP].astype(jnp.bfloat16)
    wanted = jnp.broadcast_to(targets_ref[...], (REST, EXTRA))
    first = lax.broadcasted_iota(jnp.int32, (REST, EXTRA), 0) == 0
    digits = jnp.where(first, wanted >> 8, wanted & 255)
    rl[0, 0, :, depth : depth + EXTRA] = digits.astype(jnp.float32).astype(jnp.bfloat16)
    turn[...] = jnp.zeros_like(turn)

    pl.semaphore_wait(barrier, len(near))
    for j in (1, 3, 2):
        start(y_side(j))
    for way in (0, 1):
        start([z_main(way, 1)])
    for way in (0, 1):
        start([y_main(0, way)])
    for j in (1, 3, 2):
        arrive(y_side(j))
    for way in (0, 1):
        start(z_side(way, 1))

    lane = lax.broadcasted_iota(jnp.int32, (8, 128), 1)
    sub = lax.broadcasted_iota(jnp.int32, (8, 128), 0)
    start_column = (me * vocab_dev).astype(jnp.float32)

    def fill(p, base):
        for j in range(NY):
            block[base + MAIN * j : base + MAIN * (j + 1), 0:SPLIT] = za[p, j].astype(jnp.float32)
            block[base + MAIN * j : base + MAIN * (j + 1), SPLIT:depth] = yb[p, j].astype(jnp.float32)
        for j in range(NY):
            rest32[REST * j : REST * (j + 1), :] = rl[p, j].astype(jnp.float32)
        block[base + MAIN * NY : base + CAP * NY, :] = rest32[:, 0:depth]
        digits8 = rest32[:, depth : depth + EXTRA]
        columns = []
        last = jnp.zeros((8, 128), jnp.float32)
        for j in range(NY):
            ids = digits8[2 * j : 2 * j + 1] * 256.0 + digits8[2 * j + 1 : 2 * j + 2]
            ids = jnp.broadcast_to(ids, (8, 128))
            columns.append(jnp.sum(jnp.where(lane == sub, ids, 0.0), axis=1, keepdims=True))
            last = jnp.where(sub // REST == j, ids, last)
        columns.append(jnp.sum(jnp.where(lane == MAIN + lax.rem(sub, REST), last, 0.0), axis=1, keepdims=True))
        return columns

    pair = 2 * CAP * NY

    def compute(q):
        low = q
        high = jnp.where(q == NZ // 2, 0, NZ - q)
        columns = fill(low, 0) + fill(high, CAP * NY)
        wanted_column = jnp.concatenate(columns, axis=0) - start_column
        lhs = block[...].astype(jnp.bfloat16)
        for n in range(0, vocab_dev, 256):
            logits[:, n : n + 256] = (
                jnp.dot(lhs, weight[:, n : n + 256], preferred_element_type=jnp.float32) * logit_scale
            )
        z = logits[...]
        peak = jnp.max(z, axis=1, keepdims=True)
        e = jnp.exp(z - peak)
        total = jnp.sum(e, axis=1, keepdims=True)
        moment = jnp.sum(e * z, axis=1, keepdims=True)
        column = lax.broadcasted_iota(jnp.int32, z.shape, 1).astype(jnp.float32)
        chosen = jnp.sum(jnp.where(column == wanted_column, z, 0.0), axis=1, keepdims=True)
        side = lax.broadcasted_iota(jnp.int32, (pair, 128), 1)
        turn[0:pair, :] = jnp.where(
            side == 0, peak, jnp.where(side == 1, total, jnp.where(side == 2, moment, chosen))
        )
        turned = jnp.transpose(turn[...])[0:8]
        stat_out[low] = turned
        stat_out[high] = pltpu.roll(turned, 128 - CAP * NY, 1)
        start([stat_copy(low)])

        @pl.when(q < NZ // 2)
        def _():
            start([stat_copy(high)])

    last_hop = NZ // 2

    def step(hop, carry):
        @pl.when(hop < last_hop)
        def _():
            for way in (0, 1):
                arrive([z_main(way, hop)])

            @pl.when(hop < last_hop - 1)
            def _():
                for way in (0, 1):
                    start([z_main(way, hop + 1)])

            @pl.when(hop == last_hop - 1)
            def _():
                for way in (0, 1):
                    start([z_main_half(way)])

            for p in (plane(0, hop), plane(1, hop)):
                for way in (0, 1):
                    start([y_main(p, way)])
            for way in (0, 1):
                arrive(z_side(way, hop))

            @pl.when(hop < last_hop - 1)
            def _():
                for way in (0, 1):
                    start(z_side(way, hop + 1))

            @pl.when(hop == last_hop - 1)
            def _():
                for way in (0, 1):
                    start(z_side_half(way))

        @pl.when(hop == last_hop)
        def _():
            for way in (0, 1):
                arrive([z_main_half(way)])
            for way in (0, 1):
                start([y_main(last_hop, way)])
            for way in (0, 1):
                arrive(z_side_half(way))

        @pl.when(hop <= last_hop + 1)
        def _():
            q = hop - 1

            def second(p):
                for way in (0, 1):
                    arrive([y_main(p, way)])
                    start([y_half(p, way)])

            second(q)

            @pl.when(jnp.logical_and(q > 0, q < last_hop))
            def _():
                second(NZ - q)

        @pl.when(hop == 3)
        def _():
            fetch_weight.wait()

        @pl.when(hop >= 3)
        def _():
            q = hop - 2
            for p in (q, jnp.where(q == last_hop, 0, NZ - q)):
                for way in (0, 1):
                    arrive([y_half(p, way)])
            compute(q)

        return carry

    lax.fori_loop(1, last_hop + 3, step, 0)

    def merge(peaks, totals, moments, chosens):
        peak = jnp.max(peaks, axis=0, keepdims=True)
        factor = jnp.exp(peaks - peak)
        return (
            peak,
            jnp.sum(totals * factor, axis=0, keepdims=True),
            jnp.sum(moments * factor, axis=0, keepdims=True),
            jnp.sum(chosens, axis=0, keepdims=True),
        )

    stat_in[0] = stat_out[0]

    def await_stat(p, carry):
        arrive([stat_copy(p)])
        return carry

    lax.fori_loop(1, NZ, await_stat, 0)
    peak, total, moment, chosen = merge(stat_in[:, 0], stat_in[:, 1], stat_in[:, 2], stat_in[:, 3])
    sums = jnp.where(sub == 0, peak, jnp.where(sub == 1, total, jnp.where(sub == 2, moment, chosen)))
    sum_out[...] = sums
    sum_in[0] = sums
    for j in (2, 1, 3):
        start([sum_copy(j)])
    for j in (1, 3, 2):
        arrive([sum_copy(j)])
    mine = []
    for j in range(NY):
        tile = sum_in[j]
        body = pltpu.roll(tile, (128 - MAIN * j) % 128, 1)
        tail = pltpu.roll(tile, (128 + MAIN - MAIN * NY - REST * j) % 128, 1)
        mine.append(jnp.where(lane < MAIN, body, tail))
    peak, total, moment, chosen = merge(
        *[jnp.concatenate([tile[i : i + 1] for tile in mine], axis=0) for i in range(4)]
    )
    log_total = jnp.log(total)
    scored = lax.broadcasted_iota(jnp.int32, (1, 128), 1) < counts_ref[0]
    slots = logprob_ref.shape[1]
    logprob_ref[...] = jnp.where(scored, chosen - peak - log_total, 0.0)[:, 0:slots]
    entropy_ref[...] = jnp.where(scored, peak + log_total - moment / total, 0.0)[:, 0:slots]

    for j in (1, 2, 3):
        for copy in y_side(j):
            copy.wait_send()
        sum_copy(j).wait_send()

    def sent_z(hop, carry):
        for way in (0, 1):
            z_main(way, hop).wait_send()
            for copy in z_side(way, hop):
                copy.wait_send()
        return carry

    lax.fori_loop(1, last_hop, sent_z, 0)
    for way in (0, 1):
        z_main_half(way).wait_send()
        for copy in z_side_half(way):
            copy.wait_send()

    def sent_y(p, carry):
        for way in (0, 1):
            y_main(p, way).wait_send()
            y_half(p, way).wait_send()
        return carry

    lax.fori_loop(0, NZ, sent_y, 0)

    def sent_stat(p, carry):
        stat_copy(p).wait_send()
        return carry

    lax.fori_loop(1, NZ, sent_stat, 0)


def on_device(hidden, norm_gain, head_weight, targets, counts):
    slots, depth = hidden.shape
    vocab_dev = head_weight.shape[1]
    dma = pltpu.SemaphoreType.DMA
    hops = NZ // 2 + 1
    any_spec = pl.BlockSpec(memory_space=pl.ANY)
    vmem_spec = pl.BlockSpec(memory_space=pltpu.VMEM)
    wanted = jnp.pad(targets[None, :], ((0, 0), (0, EXTRA - slots)))
    logprob, entropy = pl.pallas_call(
        kernel,
        out_shape=(
            jax.ShapeDtypeStruct((1, slots), jnp.float32),
            jax.ShapeDtypeStruct((1, slots), jnp.float32),
        ),
        in_specs=[any_spec, any_spec, any_spec, vmem_spec, pl.BlockSpec(memory_space=pltpu.SMEM)],
        out_specs=(vmem_spec, vmem_spec),
        scratch_shapes=[
            pltpu.VMEM((slots, depth), jnp.bfloat16),
            pltpu.VMEM((1, depth), jnp.float32),
            pltpu.VMEM((depth, vocab_dev), jnp.bfloat16),
            pltpu.VMEM((NZ, NY, MAIN, SPLIT), jnp.bfloat16),
            pltpu.VMEM((NZ, NY, MAIN, depth - SPLIT), jnp.bfloat16),
            pltpu.VMEM((NZ, NY, REST, depth + EXTRA), jnp.bfloat16),
            pltpu.VMEM((NY * REST, depth + EXTRA), jnp.float32),
            pltpu.VMEM((2 * NY * CAP, depth), jnp.float32),
            pltpu.VMEM((2 * NY * CAP, vocab_dev), jnp.float32),
            pltpu.VMEM((128, 128), jnp.float32),
            pltpu.VMEM((NZ, 8, 128), jnp.float32),
            pltpu.VMEM((NZ, 8, 128), jnp.float32),
            pltpu.VMEM((8, 128), jnp.float32),
            pltpu.VMEM((NY, 8, 128), jnp.float32),
            dma((3,)),
            dma((2, hops)), dma((2, hops)),
            dma((2, hops)), dma((2, hops)),
            dma((2, hops)), dma((2, hops)),
            dma((NZ, 2)), dma((NZ, 2)),
            dma((NZ, 2)), dma((NZ, 2)),
            dma((NY,)), dma((NY,)),
            dma((NY,)), dma((NY,)),
            dma((NZ,)), dma((NZ,)),
            dma((NY,)), dma((NY,)),
        ],
        compiler_params=pltpu.CompilerParams(collective_id=0, has_side_effects=True),
    )(hidden, norm_gain[None, :], head_weight, wanted, counts)
    return (logprob.reshape(slots), entropy.reshape(slots))


def solution(mesh):
    in_specs = (
        P(("req", "vocab"), None),
        P(),
        P(None, "vocab"),
        P(("req", "vocab")),
        P(("req", "vocab")),
    )
    out_specs = (P(("req", "vocab")), P(("req", "vocab")))
    return jax.shard_map(
        on_device, mesh=mesh, in_specs=in_specs, out_specs=out_specs, check_vma=False
    )
```

time: 598 us -> 75.1 us (0.13)
  blocking collectives: 448 us -> 0 us
  waiting for transfers between devices: 115 us -> 0 us
  Pallas kernels: 0 us -> 68.8 us
  between operations: 15.4 us -> 1.29 us
  matrix products: 9.76 us -> 0 us
  other arithmetic: 6.94 us -> 0 us
    psum x1 -> x0, blocking collectives: 274 us -> none  [on_device(): lax.psum((local_total * factor, local_moment * factor, local_chosen), 'vo...]
    pmax x1 -> x0, blocking collectives: 140 us -> none  [on_device(): peak = lax.pmax(local_peak, 'vocab')]
    all_gather x1 -> x0, waiting for transfers between devices: 115 us -> none  [on_device(): gathered = lax.all_gather(normed, 'vocab', axis=0, tiled=True)]
    pallas_call x0 -> x1, Pallas kernels: none -> 68.8 us  [on_device(): pl.pallas_call(kernel, out_shape=(jax.ShapeDtypeStruct((1, slots), jnp.fl...]
    unnamed x1 -> x0, blocking collectives: 34.4 us -> none
    dot_general x1 -> x0, matrix products: 9.76 us -> none  [on_device(): jnp.dot(gathered, head_weight, preferred_element_type=jnp.float32)]
  transfers between devices with their start and end apart: 1 -> 0, of which waited for: 1 -> 0; matrix products, arithmetic and copies ran while one was open for 0% -> 0% of each run, Pallas kernels for 0% -> 0%
where the time goes in v1:
time: 75.1 us; the launch traced here: 74.9 us
  Pallas kernels  68.8 us (92%)
  local copies, waits for them, and re-layouts  4.79 us (6%)
  between operations  1.29 us (2%)
    pallas_call x1, Pallas kernels, on_device(): pl.pallas_call(kernel, out_shape=(jax.ShapeDtypeStruct((1, slots), jnp.fl...  68.8 us
    unnamed x2, local copies, waits for them, and re-layouts  2.32 us

profile of v1, /device:TPU:6, one launch (start us, length us, event | category | flops | bytes accessed | tf_op | source)
XLA Modules:
  0.0 74.9 jit_solution(3391825672675745869)
XLA Ops:
  1.3 1.2 %pad.4.targets_ref = s32[1,128]{1,0:T(1,128)} pad(s32[1,16]{1,0:T(1,128)} %bitcast.3, s32[]{:T(128)} %constant.0.clone.1), padding=0_0x0_112 | pad | bytes 580 | tf_op jit(solution)/shard_map/jit(_pad)/pad | solution.py:350
  2.4 1.3 %broadcast_in_dim.6.gain_hbm = f32[1,2304]{1,0:T(1,128)} reshape(f32[2304]{0:T(1024)} %param.6) | data formatting | bytes 18432 | tf_op jit(solution)/shard_map/broadcast_in_dim | solution.py:386
  3.7 68.8 %shard_map.68 = (f32[1,16]{1,0:T(1,128)}, f32[1,16]{1,0:T(1,128)}) custom-call(bf16[16,2304]{1,0:T(8,128)(2,1)} %hidden_hbm.1, f32[1,2304]{1,0:T(1,128)} %broadcast_in_dim.6.gain_hbm, bf16[2304,1024]{1,0:T(8,128)(2,1)} %weight_hbm.1, s32[1,128]{1,0:T(1,128)} %pad.4.targets_ref, s32[1]{0:T(128)S(6)} %copy.9.counts_ref), custom_call_target="tpu_custom_call" | custom-call | tf_op jit(solution)/shard_map/pallas_call | solution.py:351
  72.5 1.1 %copy.10 = f32[16]{0:T(128)} copy(f32[16]{0:T(128)} %bitcast.5) | data formatting | bytes 128
  73.7 1.2 %copy.11 = f32[16]{0:T(128)} copy(f32[16]{0:T(128)} %bitcast.4) | data formatting | bytes 128

commit v2 on v0

v2 whole, which is shorter than its diff:
```python
import jax
import jax.numpy as jnp
from jax import lax
from jax.experimental import pallas as pl
from jax.experimental.pallas import tpu as pltpu
from jax.sharding import PartitionSpec as P

logit_scale = 256.0 / 2304.0
NY, NZ = 4, 16
CAP = 10
MAIN = 8
REST = CAP - MAIN
EXTRA = 128
ROWS = CAP * NY
LAST = NZ // 2
SOURCE = {4: 0, 1: 0, 2: 1, 6: 4, 5: 4, 3: 2, 7: 6, 8: 6}
BLOCKS = 4
WAYS = (1, -1)


def plane(way, k):
    return k * way % NZ


def kernel(
    hidden_hbm, gain_hbm, weight_hbm, targets_hbm, counts_hbm,
    out_ref,
    hid, gain, weight, ids, held, main, rest, rest32, block, logits, turn, stat_out, stat_in, sum_out, sum_in,
    local_sem, zm_s, zm_r, zr_s, zr_r, ym_s, ym_r, yh_s, yh_r, r0_s, r0_r, st_s, st_r, s2_s, s2_r,
):
    depth = hid.shape[1]
    half = depth // 2
    vocab_dev = weight.shape[1]
    me = lax.axis_index("vocab")
    my_y, my_z = me // NZ, lax.rem(me, NZ)

    def at(dy, dz):
        return {"vocab": lax.rem(my_y + dy + NY, NY) * NZ + lax.rem(my_z + dz + NZ, NZ)}

    reach = sorted({k - SOURCE[k] for k in SOURCE})
    near = [at(0, way * k) for k in reach for way in WAYS] + [at(dy, 0) for dy in range(1, NY)]
    barrier = pltpu.get_barrier_semaphore()
    for device in near:
        pl.semaphore_signal(barrier, inc=1, device_id=device, device_id_type=pl.DeviceIdType.MESH)
    fetches = [
        pltpu.make_async_copy(src, dst, local_sem.at[i])
        for i, (src, dst) in enumerate(
            [(hidden_hbm, hid), (gain_hbm, gain), (targets_hbm, ids), (counts_hbm, held), (weight_hbm, weight)]
        )
    ]
    for fetch in fetches:
        fetch.start()

    def remote(src, dst, send, recv, device):
        return pltpu.make_async_remote_copy(
            src_ref=src, dst_ref=dst, send_sem=send, recv_sem=recv,
            device_id=device, device_id_type=pl.DeviceIdType.MESH,
        )

    def z_main(way, k):
        src, dst = plane(way, SOURCE[k]), plane(way, k)
        device = at(0, way * (k - SOURCE[k]))
        if k < LAST:
            return remote(main.at[src, 0], main.at[dst, 0], zm_s.at[dst], zm_r.at[dst], device)
        cols = pl.ds(0, half) if way == 1 else pl.ds(half, half)
        sem = LAST if way == 1 else NZ
        return remote(main.at[src, 0, :, cols], main.at[dst, 0, :, cols], zm_s.at[sem], zm_r.at[sem], device)

    def z_rest(way, k):
        src, dst = plane(way, SOURCE[k]), plane(way, k)
        device = at(0, way * (k - SOURCE[k]))
        if k < LAST:
            return remote(rest.at[src], rest.at[dst], zr_s.at[dst], zr_r.at[dst], device)
        part = pl.ds(0, NY // 2) if way == 1 else pl.ds(NY // 2, NY // 2)
        sem = LAST if way == 1 else NZ
        return remote(rest.at[src, part], rest.at[dst, part], zr_s.at[sem], zr_r.at[sem], device)

    def y_main(p, way):
        slot = way % NY
        i = WAYS.index(way)
        return remote(main.at[p, 0], main.at[p, slot], ym_s.at[p, i], ym_r.at[p, i], at(way, 0))

    def y_half(p, way):
        slot = way % NY
        i = WAYS.index(way)
        cols = pl.ds(0, half) if way == 1 else pl.ds(half, half)
        return remote(
            main.at[p, slot, :, cols], main.at[p, NY // 2, :, cols], yh_s.at[p, i], yh_r.at[p, i], at(way, 0)
        )

    def y_rest(j):
        return remote(rest.at[0, 0], rest.at[0, j], r0_s.at[j], r0_r.at[j], at(j, 0))

    def stat_copy(p):
        return remote(stat_out.at[p], stat_in.at[p], st_s.at[p], st_r.at[p], at(0, -p))

    def sum_copy(j):
        return remote(sum_out, sum_in.at[j], s2_s.at[j], s2_r.at[j], at(-j, 0))

    def send_z(copy, parent):
        for k in SOURCE:
            if SOURCE[k] == parent:
                for way in WAYS:
                    copy(way, k).start()

    def planes(k):
        return (k,) if k in (0, LAST) else (plane(1, k), plane(-1, k))

    def on_main(k):
        for way in WAYS:
            z_main(way, k).wait_recv()
        send_z(z_main, k)
        fan_out(k)

    def fan_out(k):
        for p in planes(k):
            for way in WAYS:
                y_main(p, way).start()

    def on_rest(k):
        for way in WAYS:
            z_rest(way, k).wait_recv()
        send_z(z_rest, k)

    def on_y(k):
        for p in planes(k):
            for way in WAYS:
                y_main(p, way).wait_recv()
                y_half(p, way).start()

    def ready(*distances):
        for k in distances:
            for p in planes(k):
                for way in WAYS:
                    y_half(p, way).wait_recv()

    for fetch in fetches[:3]:
        fetch.wait()
    values = hid[...].astype(jnp.float32)
    square_mean = jnp.mean(values * values, axis=1, keepdims=True)
    normed = values * lax.rsqrt(square_mean + 1e-05) * gain[...][None, :]
    main[0, 0] = normed[0:MAIN].astype(jnp.bfloat16)
    rest[0, 0, :, 0:depth] = normed[MAIN:CAP].astype(jnp.bfloat16)
    place = lax.broadcasted_iota(jnp.int32, (REST, EXTRA), 1)
    wanted = jnp.zeros((REST, EXTRA), jnp.int32)
    for i in range(CAP):
        wanted = jnp.where(place == i, ids[i], wanted)
    first = lax.broadcasted_iota(jnp.int32, (REST, EXTRA), 0) == 0
    digits = jnp.where(first, wanted >> 8, wanted & 255)
    rest[0, 0, :, depth : depth + EXTRA] = digits.astype(jnp.float32).astype(jnp.bfloat16)
    turn[...] = jnp.zeros_like(turn)

    pl.semaphore_wait(barrier, len(near))
    for j in (2, 1, 3):
        y_rest(j).start()
    send_z(z_main, 0)
    fan_out(0)

    lane = lax.broadcasted_iota(jnp.int32, (8, 128), 1)
    sub = lax.broadcasted_iota(jnp.int32, (8, 128), 0)
    start_column = (me * vocab_dev).astype(jnp.float32)

    def fill(p, base):
        for j in range(NY):
            block[base + MAIN * j : base + MAIN * (j + 1), :] = main[p, j].astype(jnp.float32)
        for j in range(NY):
            rest32[REST * j : REST * (j + 1), :] = rest[p, j].astype(jnp.float32)
        block[base + MAIN * NY : base + ROWS, :] = rest32[:, 0:depth]
        digits8 = rest32[:, depth : depth + EXTRA]
        columns = []
        last = jnp.zeros((8, 128), jnp.float32)
        for j in range(NY):
            number = digits8[2 * j : 2 * j + 1] * 256.0 + digits8[2 * j + 1 : 2 * j + 2]
            number = jnp.broadcast_to(number, (8, 128))
            columns.append(jnp.sum(jnp.where(lane == sub, number, 0.0), axis=1, keepdims=True))
            last = jnp.where(sub // REST == j, number, last)
        columns.append(jnp.sum(jnp.where(lane == MAIN + lax.rem(sub, REST), last, 0.0), axis=1, keepdims=True))
        return columns

    def compute(members):
        columns = []
        for i, p in enumerate(members):
            columns += fill(p, ROWS * i)
        wanted_column = jnp.concatenate(columns, axis=0) - start_column
        lhs = block[...].astype(jnp.bfloat16)
        for n in range(0, vocab_dev, 256):
            logits[:, n : n + 256] = (
                jnp.dot(lhs, weight[:, n : n + 256], preferred_element_type=jnp.float32) * logit_scale
            )
        z = logits[...]
        peak = jnp.max(z, axis=1, keepdims=True)
        e = jnp.exp(z - peak)
        total = jnp.sum(e, axis=1, keepdims=True)
        moment = jnp.sum(e * z, axis=1, keepdims=True)
        column = lax.broadcasted_iota(jnp.int32, z.shape, 1).astype(jnp.float32)
        chosen = jnp.sum(jnp.where(column == wanted_column, z, 0.0), axis=1, keepdims=True)
        side = lax.broadcasted_iota(jnp.int32, (z.shape[0], 128), 1)
        stats = jnp.where(side == 0, peak, jnp.where(side == 1, total, jnp.where(side == 2, moment, chosen)))
        for i in range(len(members)):
            turn[64 * i : 64 * i + ROWS, :] = stats[ROWS * i : ROWS * (i + 1)]
        for i in range(0, len(members), 2):
            turned = jnp.transpose(turn[64 * i : 64 * i + 128, :])[0:8]
            stat_out[members[i]] = turned
            stat_out[members[i + 1]] = pltpu.roll(turned, 64, 1)

    on_main(1)
    for j in (1, 3, 2):
        y_rest(j).wait_recv()
    send_z(z_rest, 0)
    on_main(4)
    on_y(0)
    on_main(2)
    on_rest(1)
    on_y(1)
    on_main(6)
    on_main(5)
    on_rest(4)
    on_main(3)
    on_y(4)
    on_rest(2)
    on_y(2)
    on_main(7)
    on_main(8)
    on_rest(6)

    def group(b, carry):
        @pl.when(b == 0)
        def _():
            ready(1, 4)
            fetches[4].wait()

        @pl.when(b == 1)
        def _():
            on_y(5)
            on_y(6)
            on_y(3)
            on_y(7)
            on_y(8)
            on_rest(5)
            ready(2, 5)

        @pl.when(b == 2)
        def _():
            on_rest(3)
            ready(3, 6)

        @pl.when(b == 3)
        def _():
            on_rest(7)
            on_rest(8)
            ready(7, 8, 0)

        end = b == BLOCKS - 1
        low = jnp.where(end, 7, b + 1)
        high = jnp.where(end, LAST, b + 4)
        members = (low, NZ - low, high, jnp.where(end, 0, NZ - high))
        compute(members)
        for p in members[:3]:
            stat_copy(p).start()

        @pl.when(b < BLOCKS - 1)
        def _():
            stat_copy(members[3]).start()

        return carry

    lax.fori_loop(0, BLOCKS, group, 0)

    def merge(peaks, totals, moments, chosens):
        peak = jnp.max(peaks, axis=0, keepdims=True)
        factor = jnp.exp(peaks - peak)
        return (
            peak,
            jnp.sum(totals * factor, axis=0, keepdims=True),
            jnp.sum(moments * factor, axis=0, keepdims=True),
            jnp.sum(chosens, axis=0, keepdims=True),
        )

    stat_in[0] = stat_out[0]
    for p in range(1, NZ):
        stat_copy(p).wait_recv()
    peak, total, moment, chosen = merge(stat_in[:, 0], stat_in[:, 1], stat_in[:, 2], stat_in[:, 3])
    sums = jnp.where(sub == 0, peak, jnp.where(sub == 1, total, jnp.where(sub == 2, moment, chosen)))
    sum_out[...] = sums
    sum_in[0] = sums
    for j in (2, 1, 3):
        sum_copy(j).start()
    for j in (1, 3, 2):
        sum_copy(j).wait_recv()
    mine = []
    for j in range(NY):
        tile = sum_in[j]
        body = pltpu.roll(tile, (128 - MAIN * j) % 128, 1)
        tail = pltpu.roll(tile, (128 + MAIN - MAIN * NY - REST * j) % 128, 1)
        mine.append(jnp.where(lane < MAIN, body, tail))
    peak, total, moment, chosen = merge(
        *[jnp.concatenate([tile[i : i + 1] for tile in mine], axis=0) for i in range(4)]
    )
    log_total = jnp.log(total)
    fetches[3].wait()
    scored = lax.broadcasted_iota(jnp.int32, (1, 128), 1) < held[0]
    slots = out_ref.shape[1]
    out_ref[0:1, :] = jnp.where(scored, chosen - peak - log_total, 0.0)[:, 0:slots]
    out_ref[1:2, :] = jnp.where(scored, peak + log_total - moment / total, 0.0)[:, 0:slots]

    for j in range(1, NY):
        y_rest(j).wait_send()
        sum_copy(j).wait_send()
    for k in SOURCE:
        for way in WAYS:
            z_main(way, k).wait_send()
            z_rest(way, k).wait_send()
    for p in range(NZ):
        for way in WAYS:
            y_main(p, way).wait_send()
            y_half(p, way).wait_send()
        if p:
            stat_copy(p).wait_send()


def on_device(hidden, norm_gain, head_weight, targets, counts):
    slots, depth = hidden.shape
    vocab_dev = head_weight.shape[1]
    dma = pltpu.SemaphoreType.DMA
    any_spec = pl.BlockSpec(memory_space=pl.ANY)
    both = pl.pallas_call(
        kernel,
        out_shape=jax.ShapeDtypeStruct((2, slots), jnp.float32),
        in_specs=[any_spec] * 5,
        out_specs=pl.BlockSpec(memory_space=pltpu.VMEM),
        scratch_shapes=[
            pltpu.VMEM((slots, depth), jnp.bfloat16),
            pltpu.VMEM((depth,), jnp.float32),
            pltpu.VMEM((depth, vocab_dev), jnp.bfloat16),
            pltpu.SMEM((slots,), jnp.int32),
            pltpu.SMEM((1,), jnp.int32),
            pltpu.VMEM((NZ, NY, MAIN, depth), jnp.bfloat16),
            pltpu.VMEM((NZ, NY, REST, depth + EXTRA), jnp.bfloat16),
            pltpu.VMEM((NY * REST, depth + EXTRA), jnp.float32),
            pltpu.VMEM((BLOCKS * ROWS, depth), jnp.float32),
            pltpu.VMEM((BLOCKS * ROWS, vocab_dev), jnp.float32),
            pltpu.VMEM((256, 128), jnp.float32),
            pltpu.VMEM((NZ, 8, 128), jnp.float32),
            pltpu.VMEM((NZ, 8, 128), jnp.float32),
            pltpu.VMEM((8, 128), jnp.float32),
            pltpu.VMEM((NY, 8, 128), jnp.float32),
            dma((5,)),
            dma((NZ + 1,)), dma((NZ + 1,)),
            dma((NZ + 1,)), dma((NZ + 1,)),
            dma((NZ, 2)), dma((NZ, 2)),
            dma((NZ, 2)), dma((NZ, 2)),
            dma((NY,)), dma((NY,)),
            dma((NZ,)), dma((NZ,)),
            dma((NY,)), dma((NY,)),
        ],
        compiler_params=pltpu.CompilerParams(collective_id=0, has_side_effects=True),
    )(hidden, norm_gain, head_weight, targets, counts)
    return (both[0], both[1])


def solution(mesh):
    in_specs = (
        P(("req", "vocab"), None),
        P(),
        P(None, "vocab"),
        P(("req", "vocab")),
        P(("req", "vocab")),
    )
    out_specs = (P(("req", "vocab")), P(("req", "vocab")))
    return jax.shard_map(
        on_device, mesh=mesh, in_specs=in_specs, out_specs=out_specs, check_vma=False
    )
```

time: 598 us -> 61.6 us (0.10)
  blocking collectives: 448 us -> 0 us
  waiting for transfers between devices: 115 us -> 0 us
  Pallas kernels: 0 us -> 58.9 us
  between operations: 15.4 us -> 1.29 us
  matrix products: 9.76 us -> 0 us
  other arithmetic: 6.94 us -> 0 us
    psum x1 -> x0, blocking collectives: 274 us -> none  [on_device(): lax.psum((local_total * factor, local_moment * factor, local_chosen), 'vo...]
    pmax x1 -> x0, blocking collectives: 140 us -> none  [on_device(): peak = lax.pmax(local_peak, 'vocab')]
    all_gather x1 -> x0, waiting for transfers between devices: 115 us -> none  [on_device(): gathered = lax.all_gather(normed, 'vocab', axis=0, tiled=True)]
    pallas_call x0 -> x1, Pallas kernels: none -> 58.9 us  [on_device(): pl.pallas_call(kernel, out_shape=jax.ShapeDtypeStruct((2, slots), jnp.flo...]
    unnamed x1 -> x0, blocking collectives: 34.4 us -> none
    dot_general x1 -> x0, matrix products: 9.76 us -> none  [on_device(): jnp.dot(gathered, head_weight, preferred_element_type=jnp.float32)]
  transfers between devices with their start and end apart: 1 -> 0, of which waited for: 1 -> 0; matrix products, arithmetic and copies ran while one was open for 0% -> 0% of each run, Pallas kernels for 0% -> 0%
where the time goes in v2:
time: 61.6 us; the launch traced here: 61.5 us
  Pallas kernels  58.9 us (96%)
  between operations  1.29 us (2%)
  local copies, waits for them, and re-layouts  1.25 us (2%)
    pallas_call x1, Pallas kernels, on_device(): pl.pallas_call(kernel, out_shape=jax.ShapeDtypeStruct((2, slots), jnp.flo...  58.9 us
    squeeze x1, local copies, waits for them, and re-layouts, on_device(): return (both[0], both[1])  1.25 us

profile of v2, /device:TPU:6, one launch (start us, length us, event | category | flops | bytes accessed | tf_op | source)
XLA Modules:
  0.0 61.5 jit_solution(17177981232531402886)
XLA Ops:
  1.3 58.9 %shard_map.68 = f32[2,16]{1,0:T(2,128)} custom-call(bf16[16,2304]{1,0:T(8,128)(2,1)} %hidden_hbm.1, f32[2304]{0:T(1024)} %gain_hbm.1, bf16[2304,1024]{1,0:T(8,128)(2,1)} %weight_hbm.1, s32[16]{0:T(128)} %targets_hbm.1, s32[1]{0:T(128)S(6)} %copy.7.counts_hbm), custom_call_target="tpu_custom_call" | custom-call | tf_op jit(solution)/shard_map/pallas_call | solution.py:326
  60.2 1.3 %slice_bitcast_fusion = (f32[16]{0:T(128)}, f32[16]{0:T(128)}) fusion(f32[2,16]{1,0:T(2,128)} %shard_map.68), kind=kLoop, calls=%fused_computation | loop fusion | bytes 256 | tf_op jit(solution)/shard_map/squeeze | solution.py:358

commit v3 on v2

v3 whole, which is shorter than its diff:
```python
import jax
import jax.numpy as jnp
from jax import lax
from jax.experimental import pallas as pl
from jax.experimental.pallas import tpu as pltpu
from jax.sharding import PartitionSpec as P

logit_scale = 256.0 / 2304.0
NY, NZ = 4, 16
CAP = 10
MAIN = 8
REST = CAP - MAIN
EXTRA = 128
ROWS = CAP * NY
LANES = 32
LAST = NZ // 2
SOURCE = {1: 0, 3: 0, 2: 1, 6: 3, 4: 3, 8: 6, 7: 6, 5: 6}
REST_FIRST = (3, 1, 2, 6, 4, 8, 7, 5)
DIRECT = ()
GROUPS = ((3, 13, 2, 14), (6, 10, 4, 12), (7, 9, 8, 11), (0, 1, 15, 5))
ORDER = (
    ("m1", "y0", "Y", "m3", "m2", "y1", "y3", "m6", "m4", "r3", "r1", "y2", "m7", "m5", "m8", "r2", "c2", "c3"),
    ("y6", "r6", "y4", "y7", "y8", "y5", "r4", "c6", "c4"),
    ("c7", "c8", "c5", "r5", "r7", "r8"),
    ("c0", "c1"),
)
WAYS = (1, -1)


def plane(way, k):
    return k * way % NZ


def kernel(
    hidden_hbm, gain_hbm, weight_hbm, targets_hbm, counts_hbm,
    out_ref,
    hid, gain, weight, ids, held, main, rest, rest32, block, logits, stat_out, stat_in,
    local_sem, zm_s, zm_r, zr_s, zr_r, ym_s, ym_r, yh_s, yh_r, r0_s, r0_r, st_s, st_r,
):
    depth = hid.shape[1]
    half = depth // 2
    vocab_dev = weight.shape[1]
    me = lax.axis_index("vocab")
    my_y, my_z = me // NZ, lax.rem(me, NZ)

    def at(dy, dz):
        return {"vocab": lax.rem(my_y + dy + NY, NY) * NZ + lax.rem(my_z + dz + NZ, NZ)}

    reach = sorted({abs(k - SOURCE[k]) for k in SOURCE})
    near = [at(0, way * k) for k in reach for way in WAYS] + [at(dy, 0) for dy in range(1, NY)]
    barrier = pltpu.get_barrier_semaphore()
    for device in near:
        pl.semaphore_signal(barrier, inc=1, device_id=device, device_id_type=pl.DeviceIdType.MESH)
    fetches = [
        pltpu.make_async_copy(src, dst, local_sem.at[i])
        for i, (src, dst) in enumerate(
            [(hidden_hbm, hid), (gain_hbm, gain), (targets_hbm, ids), (counts_hbm, held), (weight_hbm, weight)]
        )
    ]
    for fetch in fetches:
        fetch.start()

    def remote(src, dst, send, recv, device):
        return pltpu.make_async_remote_copy(
            src_ref=src, dst_ref=dst, send_sem=send, recv_sem=recv,
            device_id=device, device_id_type=pl.DeviceIdType.MESH,
        )

    def z_main(way, k):
        src, dst = plane(way, SOURCE[k]), plane(way, k)
        device = at(0, way * (k - SOURCE[k]))
        if k < LAST:
            return remote(main.at[src, 0], main.at[dst, 0], zm_s, zm_r.at[k], device)
        cols = pl.ds(0, half) if way == 1 else pl.ds(half, half)
        return remote(main.at[src, 0, :, cols], main.at[dst, 0, :, cols], zm_s, zm_r.at[k], device)

    def z_rest(way, k):
        src, dst = plane(way, SOURCE[k]), plane(way, k)
        device = at(0, way * (k - SOURCE[k]))
        if k < LAST:
            return remote(rest.at[src], rest.at[dst], zr_s, zr_r.at[k], device)
        part = pl.ds(0, NY // 2) if way == 1 else pl.ds(NY // 2, NY // 2)
        return remote(rest.at[src, part], rest.at[dst, part], zr_s, zr_r.at[k], device)

    def y_main(p, way):
        return remote(main.at[p, 0], main.at[p, way % NY], ym_s, ym_r.at[distance(p)], at(way, 0))

    def y_far(p):
        return remote(main.at[p, 0], main.at[p, NY // 2], ym_s, ym_r.at[distance(p)], at(NY // 2, 0))

    def y_half(p, way):
        cols = pl.ds(0, half) if way == 1 else pl.ds(half, half)
        return remote(
            main.at[p, way % NY, :, cols], main.at[p, NY // 2, :, cols], yh_s, yh_r.at[distance(p)], at(way, 0)
        )

    def y_rest(j):
        return remote(rest.at[0, 0], rest.at[0, j], r0_s, r0_r, at(j, 0))

    def stat_copy(p, j):
        return remote(stat_out.at[p, j], stat_in.at[p * NY + j], st_s, st_r, at(-j, -p))

    def arrive(view, sem):
        remote(view, view, local_sem.at[0], sem, at(1, 0)).wait_recv()

    def left(view, sem):
        remote(view, view, sem, local_sem.at[0], at(1, 0)).wait_send()

    def distance(p):
        return min(p, NZ - p)

    def planes(k):
        return (k,) if k in (0, LAST) else (plane(1, k), plane(-1, k))

    def send_z(copy, parent):
        for k in REST_FIRST if copy is z_rest else SOURCE:
            if SOURCE[k] == parent:
                for way in WAYS:
                    copy(way, k).start()

    def fan_out(k):
        for p in planes(k):
            if k in DIRECT:
                y_far(p).start()
            for way in WAYS:
                y_main(p, way).start()

    def on_main(k):
        arrive(main.at[pl.ds(0, len(planes(k))), 0], zm_r.at[k])
        send_z(z_main, k)
        fan_out(k)

    def on_rest(k):
        arrive(rest.at[pl.ds(0, len(planes(k)))], zr_r.at[k])
        send_z(z_rest, k)

    def on_own_rest():
        arrive(rest.at[0, pl.ds(1, NY - 1)], r0_r)
        send_z(z_rest, 0)

    def on_y(k):
        arrive(main.at[0, pl.ds(0, 2 * len(planes(k)))], ym_r.at[k])
        for p in planes(k):
            for way in WAYS:
                y_half(p, way).start()

    def complete(k):
        if k in DIRECT:
            arrive(main.at[pl.ds(0, len(planes(k))), pl.ds(0, NY - 1)], ym_r.at[k])
        else:
            arrive(main.at[pl.ds(0, len(planes(k))), NY // 2], yh_r.at[k])

    def follow(order):
        for word in order:
            if word == "Y":
                on_own_rest()
            else:
                {"m": on_main, "r": on_rest, "y": on_y, "c": complete}[word[0]](int(word[1:]))

    for fetch in fetches[:3]:
        fetch.wait()
    values = hid[...].astype(jnp.float32)
    square_mean = jnp.mean(values * values, axis=1, keepdims=True)
    normed = values * lax.rsqrt(square_mean + 1e-05) * gain[...][None, :]
    main[0, 0] = normed[0:MAIN].astype(jnp.bfloat16)
    rest[0, 0, :, 0:depth] = normed[MAIN:CAP].astype(jnp.bfloat16)
    place = lax.broadcasted_iota(jnp.int32, (REST, EXTRA), 1)
    wanted = jnp.zeros((REST, EXTRA), jnp.int32)
    for i in range(CAP):
        wanted = jnp.where(place == i, ids[i], wanted)
    first = lax.broadcasted_iota(jnp.int32, (REST, EXTRA), 0) == 0
    digits = jnp.where(first, wanted >> 8, wanted & 255)
    rest[0, 0, :, depth : depth + EXTRA] = digits.astype(jnp.float32).astype(jnp.bfloat16)

    pl.semaphore_wait(barrier, len(near))
    for j in (2, 1, 3):
        y_rest(j).start()
    send_z(z_main, 0)
    fan_out(0)

    lane = lax.broadcasted_iota(jnp.int32, (8, 128), 1)
    sub = lax.broadcasted_iota(jnp.int32, (8, 128), 0)
    start_column = (me * vocab_dev).astype(jnp.float32)

    def fill(p, base):
        for j in range(NY):
            block[base + MAIN * j : base + MAIN * (j + 1), :] = main[p, j].astype(jnp.float32)
        for j in range(NY):
            rest32[REST * j : REST * (j + 1), :] = rest[p, j].astype(jnp.float32)
        block[base + MAIN * NY : base + ROWS, :] = rest32[:, 0:depth]
        digits8 = rest32[:, depth : depth + EXTRA]
        columns = []
        last = jnp.zeros((8, 128), jnp.float32)
        for j in range(NY):
            number = digits8[2 * j : 2 * j + 1] * 256.0 + digits8[2 * j + 1 : 2 * j + 2]
            number = jnp.broadcast_to(number, (8, 128))
            columns.append(jnp.sum(jnp.where(lane == sub, number, 0.0), axis=1, keepdims=True))
            last = jnp.where(sub // REST == j, number, last)
        columns.append(jnp.sum(jnp.where(lane == MAIN + lax.rem(sub, REST), last, 0.0), axis=1, keepdims=True))
        return columns

    def compute(members):
        columns = []
        for i, p in enumerate(members):
            columns += fill(p, ROWS * i)
        wanted_column = jnp.concatenate(columns, axis=0) - start_column
        lhs = block[...].astype(jnp.bfloat16)
        for n in range(0, vocab_dev, 256):
            logits[:, n : n + 256] = (
                jnp.dot(lhs, weight[:, n : n + 256], preferred_element_type=jnp.float32) * logit_scale
            )
        z = logits[...]
        peak = jnp.max(z, axis=1, keepdims=True)
        e = jnp.exp(z - peak)
        total = jnp.sum(e, axis=1, keepdims=True)
        moment = jnp.sum(e * z, axis=1, keepdims=True)
        column = lax.broadcasted_iota(jnp.int32, z.shape, 1).astype(jnp.float32)
        chosen = jnp.sum(jnp.where(column == wanted_column, z, 0.0), axis=1, keepdims=True)
        stats = (peak, total, moment, chosen)
        for i, p in enumerate(members):
            chunks = [[stat[ROWS * i + 8 * c : ROWS * i + 8 * (c + 1)] for stat in stats] for c in range(NY + 1)]
            last = jnp.zeros((8, 128), jnp.float32)
            for n, stat in enumerate(chunks[NY]):
                last = jnp.where(lane == LANES * n + MAIN + lax.rem(sub, REST), stat, last)
            for j in range(NY):
                tile = jnp.where(sub // REST == j, last, 0.0)
                for n, stat in enumerate(chunks[j]):
                    tile = jnp.where(lane == LANES * n + sub, stat, tile)
                stat_out[p, j] = jnp.sum(tile, axis=0, keepdims=True)

    def group(b, carry):
        for i, members in enumerate(GROUPS):

            @pl.when(b == i)
            def _():
                follow(ORDER[i])
                if i == 0:
                    fetches[4].wait()

        members = []
        for i in range(len(GROUPS[0])):
            p = jnp.int32(GROUPS[0][i])
            for j in range(1, len(GROUPS)):
                p = jnp.where(b == j, GROUPS[j][i], p)
            members.append(p)
        compute(members)
        for i, p in enumerate(members):
            for j in range(NY):
                if (i, j) != (0, 0):
                    stat_copy(p, j).start()

        @pl.when(b < len(GROUPS) - 1)
        def _():
            stat_copy(members[0], 0).start()

        return carry

    lax.fori_loop(0, len(GROUPS), group, 0)

    left(rest.at[0, pl.ds(1, NY - 1)], r0_s)
    left(main.at[pl.ds(0, NZ - 1), 0], zm_s)
    left(rest.at[pl.ds(0, NZ - 1)], zr_s)
    far = sum(len(planes(k)) for k in DIRECT)
    left(main.at[pl.ds(0, NZ), pl.ds(0, 2)], ym_s)
    if far:
        left(main.at[pl.ds(0, far), 0], ym_s)
    left(main.at[pl.ds(0, NZ - far), 0], yh_s)

    stat_in[0] = stat_out[0, 0]
    arrive(stat_in.at[pl.ds(1, NY * NZ - 1)], st_r)
    parts = stat_in[...].reshape(NY * NZ, 128)
    peak = jnp.max(parts, axis=0, keepdims=True)
    factor = jnp.exp(parts - peak)
    spot = lax.broadcasted_iota(jnp.int32, parts.shape, 1) // LANES
    factor = jnp.where(
        spot == 1,
        pltpu.roll(factor, LANES, 1),
        jnp.where(spot == 2, pltpu.roll(factor, 2 * LANES, 1), 1.0),
    )
    sums = jnp.broadcast_to(jnp.sum(parts * factor, axis=0, keepdims=True), (8, 128))
    total, moment, chosen = [pltpu.roll(sums, 128 - LANES * n, 1)[0:1] for n in (1, 2, 3)]
    log_total = jnp.log(total)
    fetches[3].wait()
    scored = lax.broadcasted_iota(jnp.int32, (1, 128), 1) < held[0]
    slots = out_ref.shape[1]
    out_ref[0:1, :] = jnp.where(scored, chosen - peak - log_total, 0.0)[:, 0:slots]
    out_ref[1:2, :] = jnp.where(scored, peak + log_total - moment / total, 0.0)[:, 0:slots]
    left(stat_in.at[pl.ds(1, NY * NZ - 1)], st_s)


def on_device(hidden, norm_gain, head_weight, targets, counts):
    slots, depth = hidden.shape
    vocab_dev = head_weight.shape[1]
    dma = pltpu.SemaphoreType.DMA
    any_spec = pl.BlockSpec(memory_space=pl.ANY)
    both = pl.pallas_call(
        kernel,
        out_shape=jax.ShapeDtypeStruct((2, slots), jnp.float32),
        in_specs=[any_spec] * 5,
        out_specs=pl.BlockSpec(memory_space=pltpu.VMEM),
        scratch_shapes=[
            pltpu.VMEM((slots, depth), jnp.bfloat16),
            pltpu.VMEM((depth,), jnp.float32),
            pltpu.VMEM((depth, vocab_dev), jnp.bfloat16),
            pltpu.SMEM((slots,), jnp.int32),
            pltpu.SMEM((1,), jnp.int32),
            pltpu.VMEM((NZ, NY, MAIN, depth), jnp.bfloat16),
            pltpu.VMEM((NZ, NY, REST, depth + EXTRA), jnp.bfloat16),
            pltpu.VMEM((NY * REST, depth + EXTRA), jnp.float32),
            pltpu.VMEM((4 * ROWS, depth), jnp.float32),
            pltpu.VMEM((4 * ROWS, vocab_dev), jnp.float32),
            pltpu.VMEM((NZ, NY, 1, 128), jnp.float32),
            pltpu.VMEM((NZ * NY, 1, 128), jnp.float32),
            dma((5,)),
            dma, dma((LAST + 1,)),
            dma, dma((LAST + 1,)),
            dma, dma((LAST + 1,)),
            dma, dma((LAST + 1,)),
            dma, dma,
            dma, dma,
        ],
        compiler_params=pltpu.CompilerParams(collective_id=0, has_side_effects=True),
    )(hidden, norm_gain, head_weight, targets, counts)
    return (both[0], both[1])


def solution(mesh):
    in_specs = (
        P(("req", "vocab"), None),
        P(),
        P(None, "vocab"),
        P(("req", "vocab")),
        P(("req", "vocab")),
    )
    out_specs = (P(("req", "vocab")), P(("req", "vocab")))
    return jax.shard_map(
        on_device, mesh=mesh, in_specs=in_specs, out_specs=out_specs, check_vma=False
    )
```

time: 61.6 us -> 53.4 us (0.87)
  Pallas kernels: 58.9 us -> 50.7 us
    pallas_call x1, Pallas kernels: 58.9 us -> 50.7 us  [on_device(): pl.pallas_call(kernel, out_shape=jax.ShapeDtypeStruct((2, slots), jnp.flo...]
where the time goes in v3:
time: 53.4 us; the launch traced here: 53.2 us
  Pallas kernels  50.7 us (95%)
  between operations  1.29 us (2%)
  local copies, waits for them, and re-layouts  1.25 us (2%)
    pallas_call x1, Pallas kernels, on_device(): pl.pallas_call(kernel, out_shape=jax.ShapeDtypeStruct((2, slots), jnp.flo...  50.7 us
    squeeze x1, local copies, waits for them, and re-layouts, on_device(): return (both[0], both[1])  1.25 us

profile of v3, /device:TPU:6, one launch (start us, length us, event | category | flops | bytes accessed | tf_op | source)
XLA Modules:
  0.0 53.2 jit_solution(609598458008939861)
XLA Ops:
  1.3 50.7 %shard_map.68 = f32[2,16]{1,0:T(2,128)} custom-call(bf16[16,2304]{1,0:T(8,128)(2,1)} %hidden_hbm.1, f32[2304]{0:T(1024)} %gain_hbm.1, bf16[2304,1024]{1,0:T(8,128)(2,1)} %weight_hbm.1, s32[16]{0:T(128)} %targets_hbm.1, s32[1]{0:T(128)S(6)} %copy.7.counts_hbm), custom_call_target="tpu_custom_call" | custom-call | tf_op jit(solution)/shard_map/pallas_call | solution.py:296
  52.0 1.3 %slice_bitcast_fusion = (f32[16]{0:T(128)}, f32[16]{0:T(128)}) fusion(f32[2,16]{1,0:T(2,128)} %shard_map.68), kind=kLoop, calls=%fused_computation | loop fusion | bytes 256 | tf_op jit(solution)/shard_map/squeeze | solution.py:324

commit v4 on v3

--- a/solution.py
+++ b/solution.py
@@ -14,15 +14,14 @@
 ROWS = CAP * NY
 LANES = 32
 LAST = NZ // 2
-SOURCE = {1: 0, 3: 0, 2: 1, 6: 3, 4: 3, 8: 6, 7: 6, 5: 6}
-REST_FIRST = (3, 1, 2, 6, 4, 8, 7, 5)
-DIRECT = ()
-GROUPS = ((3, 13, 2, 14), (6, 10, 4, 12), (7, 9, 8, 11), (0, 1, 15, 5))
+SOURCE = {2: 0, 1: 0, 4: 2, 3: 2, 6: 4, 5: 4, 8: 6, 7: 6}
+DIRECT = (7, 8)
+GROUPS = ((1, 15, 2, 14), (3, 13, 4, 12), (7, 9, 8, 6), (0, 5, 11, 10))
 ORDER = (
-    ("m1", "y0", "Y", "m3", "m2", "y1", "y3", "m6", "m4", "r3", "r1", "y2", "m7", "m5", "m8", "r2", "c2", "c3"),
-    ("y6", "r6", "y4", "y7", "y8", "y5", "r4", "c6", "c4"),
-    ("c7", "c8", "c5", "r5", "r7", "r8"),
-    ("c0", "c1"),
+    ("m2", "m1", "y0", "Y", "m4", "s1", "y1", "m3", "y2", "r2", "m6", "s3", "m5", "y4", "y3", "r4", "m8", "m7", "y6", "s5", "r1", "c1", "c2"),
+    ("r6", "s7", "y5", "r3", "c4", "c3"),
+    ("c7", "c8", "c6", "r7", "r8"),
+    ("c0", "c5", "r5"),
 )
 WAYS = (1, -1)
 
@@ -112,11 +111,15 @@
     def planes(k):
         return (k,) if k in (0, LAST) else (plane(1, k), plane(-1, k))
 
-    def send_z(copy, parent):
-        for k in REST_FIRST if copy is z_rest else SOURCE:
-            if SOURCE[k] == parent:
+    def send_z(copy, parent, odd=True):
+        for k in SOURCE:
+            if SOURCE[k] == parent and (odd or k % 2 == 0):
                 for way in WAYS:
                     copy(way, k).start()
+
+    def send_rest(k):
+        for way in WAYS:
+            z_rest(way, k).start()
 
     def fan_out(k):
         for p in planes(k):
@@ -132,11 +135,11 @@
 
     def on_rest(k):
         arrive(rest.at[pl.ds(0, len(planes(k)))], zr_r.at[k])
-        send_z(z_rest, k)
+        send_z(z_rest, k, odd=False)
 
     def on_own_rest():
         arrive(rest.at[0, pl.ds(1, NY - 1)], r0_r)
-        send_z(z_rest, 0)
+        send_z(z_rest, 0, odd=False)
 
     def on_y(k):
         arrive(main.at[0, pl.ds(0, 2 * len(planes(k)))], ym_r.at[k])
@@ -155,7 +158,7 @@
             if word == "Y":
                 on_own_rest()
             else:
-                {"m": on_main, "r": on_rest, "y": on_y, "c": complete}[word[0]](int(word[1:]))
+                {"m": on_main, "r": on_rest, "s": send_rest, "y": on_y, "c": complete}[word[0]](int(word[1:]))
 
     for fetch in fetches[:3]:
         fetch.wait()

time: 53.4 us -> 51.6 us (0.966)
  Pallas kernels: 50.7 us -> 48.9 us
    pallas_call x1, Pallas kernels: 50.7 us -> 48.9 us  [on_device(): pl.pallas_call(kernel, out_shape=jax.ShapeDtypeStruct((2, slots), jnp.flo...]
where the time goes in v4:
time: 51.6 us; the launch traced here: 51.5 us
  Pallas kernels  48.9 us (95%)
  between operations  1.29 us (2%)
  local copies, waits for them, and re-layouts  1.25 us (2%)
    pallas_call x1, Pallas kernels, on_device(): pl.pallas_call(kernel, out_shape=jax.ShapeDtypeStruct((2, slots), jnp.flo...  48.9 us
    squeeze x1, local copies, waits for them, and re-layouts, on_device(): return (both[0], both[1])  1.25 us

profile of v4, /device:TPU:6, one launch (start us, length us, event | category | flops | bytes accessed | tf_op | source)
XLA Modules:
  0.0 51.5 jit_solution(17784875099111473483)
XLA Ops:
  1.3 48.9 %shard_map.68 = f32[2,16]{1,0:T(2,128)} custom-call(bf16[16,2304]{1,0:T(8,128)(2,1)} %hidden_hbm.1, f32[2304]{0:T(1024)} %gain_hbm.1, bf16[2304,1024]{1,0:T(8,128)(2,1)} %weight_hbm.1, s32[16]{0:T(128)} %targets_hbm.1, s32[1]{0:T(128)S(6)} %copy.7.counts_hbm), custom_call_target="tpu_custom_call" | custom-call | tf_op jit(solution)/shard_map/pallas_call | solution.py:299
  50.2 1.3 %slice_bitcast_fusion = (f32[16]{0:T(128)}, f32[16]{0:T(128)}) fusion(f32[2,16]{1,0:T(2,128)} %shard_map.68), kind=kLoop, calls=%fused_computation | loop fusion | bytes 256 | tf_op jit(solution)/shard_map/squeeze | solution.py:327
